TPU v7x, 256 devices: a whole 4x4x8 slice. The times are simulated.
256 devices in a mesh: grp: 16 (over x, z_lo, core), row: 4 (over z_hi), col: 4 (over y).
Axes of the slice: x: 4, y: 4, z: 8 (z_hi: 4, z_lo: 2; z = z_hi * 2 + z_lo), core: 2. Of those that a mesh axis runs over, the one named last changes fastest.
Arguments:
- volume: float32 [32, 32, 32, 512], P(None, 'grp', 'row', 'col'), may hold values from -6 to 6
- forcing: float32 [32, 32, 32, 512], P(None, 'grp', 'row', 'col'), may hold values from -6 to 6
- medium: float32 [2, 32, 32, 512], P(None, 'grp', 'row', 'col'), may hold values from 0.5 to 3
- points: float32 [3, 32768], P(None, ('grp', 'row', 'col')), may hold values from 0 to 4
- weights: float32 [32768], P(('grp', 'row', 'col')), may hold values from 0.05 to 0.5
- cell_map: int32 [32768], P(('grp', 'row', 'col')), may hold values from 0 to 2047
- near_list: int32 [256, 256], replicated, may hold values from 0 to 1, as said below
Outputs:
- new_volume: float32 [32, 32, 32, 512], P(None, 'grp', 'row', 'col')
- potential: float32 [32, 32768], P(None, ('grp', 'row', 'col'))
Inputs may be any that keep to these rules, and one draw needn't show every extreme that they name: cell_map[p] numbers a cell of tile p // 128 in row-major order of the tile's 2 x 8 x 128 cells. near_list[i, j] = 1 lists cluster j as near to cluster i; every cluster lists itself, and how many clusters a cluster lists differs from cluster to cluster.
All inputs are finite; a program needn't handle non-finite values.
Results may differ from a plain program's by a relative error of at most 0.0041.
Values may be sent and summed in bfloat16 or wider, within the bound.
No kernel may reach another device: no remote copies, remote signals or barrier semaphores. Data moves between devices by JAX's collectives and lax.ppermute only.
A program may use at most 64 MiB of HBM per device.

v0:
```python
import jax
import jax.numpy as jnp
from jax import lax
from jax.sharding import PartitionSpec as P

RHS = 16
CX = 2
CY = 8
CZ = 128
CH = 32


FOUR_PI = 4.0 * 3.141592653589793
WAVENUMBER = 10.0
SOFTENING = 0.01
RELAX_RATE = 0.8
COUPLING = 0.5
CONTRACT = (((1,), (1,)), ((), ()))


def padded_2(x, sides, width):
    for axis, dim in sides:
        size, length = (lax.axis_size(axis), x.shape[dim])
        up = [(i, (i + 1) % size) for i in range(size - 1)]
        down = [(j, i) for i, j in up]
        last = lax.slice_in_dim(x, length - width, length, axis=dim)
        first = lax.slice_in_dim(x, 0, width, axis=dim)
        before = lax.ppermute(last, axis, up)
        after = lax.ppermute(first, axis, down)
        x = jnp.concatenate([before, x, after], axis=dim)
    return x


def helmholtz(volume, medium):
    padded = padded_2(volume, (("grp", 1), ("row", 2), ("col", 3)), 1)
    beside = padded[:, 2:, 1:-1, 1:-1] + padded[:, :-2, 1:-1, 1:-1]
    beside = beside + padded[:, 1:-1, 2:, 1:-1] + padded[:, 1:-1, :-2, 1:-1]
    beside = beside + padded[:, 1:-1, 1:-1, 2:] + padded[:, 1:-1, 1:-1, :-2]
    laplace = 6.0 * volume - beside
    real_in = volume[:RHS]
    imag_in = volume[RHS:]
    real_out = laplace[:RHS] - medium[0] * real_in + medium[1] * imag_in
    imag_out = laplace[RHS:] - medium[0] * imag_in - medium[1] * real_in
    return jnp.concatenate([real_out, imag_out], 0)


def kernel_tiles(targets, sources, listed):
    delta_x = targets[0][:, None] - sources[0][None, :]
    delta_y = targets[1][:, None] - sources[1][None, :]
    delta_z = targets[2][:, None] - sources[2][None, :]
    distance = jnp.sqrt(delta_x * delta_x + delta_y * delta_y + delta_z * delta_z + SOFTENING)
    factor = listed / (FOUR_PI * distance)
    tile_real = (jnp.cos(WAVENUMBER * distance) * factor).astype(jnp.bfloat16)
    tile_imag = (jnp.sin(WAVENUMBER * distance) * factor).astype(jnp.bfloat16)
    return (tile_real, tile_imag)


def complex_product(real_sum, imag_sum):
    return jnp.concatenate([real_sum[:RHS] - imag_sum[RHS:], real_sum[RHS:] + imag_sum[:RHS]], 0)


def block_clusters(clusters, cluster_size, limit):
    chosen = 1
    for trial in range(1, clusters + 1):
        if clusters % trial == 0 and trial * cluster_size <= limit:
            chosen = trial
    return chosen


def on_device(volume, forcing, medium, points, weights, cell_map, near_list):
    residual = forcing - helmholtz(volume, medium)
    relaxed = volume + RELAX_RATE * residual / (6.0 - medium[0])[None]
    flat = relaxed.reshape(CH, CX * CY * CZ)
    traces = (jnp.take(flat, cell_map, axis=1) * weights[None, :]).astype(jnp.bfloat16)
    group_count = lax.axis_size("grp") * lax.axis_size("row")
    column_count = lax.axis_size("col")
    group_index = lax.axis_index("grp") * lax.axis_size("row") + lax.axis_index("row")
    column_index = lax.axis_index("col")
    near_blocks = near_list.reshape(group_count, column_count, group_count, column_count)
    cluster = points.shape[1]
    own_cols = lax.dynamic_index_in_dim(near_blocks, column_index, 1, keepdims=False)
    own_cols = lax.dynamic_index_in_dim(own_cols, group_index, 1, keepdims=False)
    targets = lax.all_gather(points, ("grp", "row"), axis=1, tiled=True)
    sources = lax.all_gather(points, "col", axis=1, tiled=True)
    source_traces = lax.all_gather(traces, "col", axis=1, tiled=True)
    target_count = targets.shape[1]
    source_count = sources.shape[1]
    step_clusters = block_clusters(group_count, cluster, 1024)
    block_points = step_clusters * cluster

    def one_block(turn, partial_value):
        begin = turn * block_points
        block_targets = lax.dynamic_slice_in_dim(targets, begin, block_points, 1)
        flags = lax.dynamic_slice_in_dim(own_cols, turn * step_clusters, step_clusters, 0)
        listed = jnp.broadcast_to(
            flags[:, None, :, None].astype(jnp.float32),
            (step_clusters, cluster, column_count, cluster),
        )
        listed = listed.reshape(block_points, source_count)
        tile_real, tile_imag = kernel_tiles(block_targets, sources, listed)
        real_part = lax.dot_general(
            source_traces, tile_real, CONTRACT, preferred_element_type=jnp.float32
        )
        imag_part = lax.dot_general(
            source_traces, tile_imag, CONTRACT, preferred_element_type=jnp.float32
        )
        return lax.dynamic_update_slice_in_dim(
            partial_value, complex_product(real_part, imag_part), begin, 1
        )

    partial_value = lax.fori_loop(
        0, group_count // step_clusters, one_block, jnp.zeros((CH, target_count), jnp.float32)
    )
    potential = lax.psum_scatter(partial_value, ("grp", "row"), scatter_dimension=1, tiled=True)
    spread = jnp.zeros((CH, CX * CY * CZ), jnp.float32).at[:, cell_map].add(potential)
    new_volume = relaxed + COUPLING * spread.reshape(relaxed.shape)
    return (new_volume, potential)


def solution(mesh):
    return jax.shard_map(
        on_device,
        mesh=mesh,
        in_specs=(
            P(None, "grp", "row", "col"),
            P(None, "grp", "row", "col"),
            P(None, "grp", "row", "col"),
            P(None, ("grp", "row", "col")),
            P(("grp", "row", "col")),
            P(("grp", "row", "col")),
            P(),
        ),
        out_specs=(P(None, "grp", "row", "col"), P(None, ("grp", "row", "col"))),
        check_vma=False,
    )
```

profile of v0, /device:TPU:1, one launch (start us, length us, event | category | flops | bytes accessed | tf_op | source)
XLA Modules:
  0.0 648.6 jit_solution(6016588470859238868)
XLA Ops:
  7.2 1.0 fusion.19
  8.2 4.9 collective-permute-start.1
  13.1 1.9 collective-permute-start
  15.1 1.3 subtract_bitcast_fusion
  17.0 1.2 compare_and_fusion
  18.3 10.9 %reshape.33 = s32[64,4,64,4]{3,2,1,0:T(8,128)} reshape(s32[256,256]{1,0:T(8,128)} %param.15) | data formatting | bytes 524288 | tf_op jit(solution)/shard_map/reshape | solution.py:79
  29.2 1.6 constant_dynamic-slice_fusion.1
  31.8 1.3 collective-permute-start.2
  33.1 5.5 collective-permute-start.3
  41.1 1.3 collective-permute-start.4
  42.4 4.6 collective-permute-start.5
  47.0 136.7 %all_gather.9 = f32[3,8192]{1,0:T(4,128)} all-gather(f32[3,128]{1,0:T(4,128)S(1)} %copy-done.7), channel_id=1, replica_groups=mesh['grp'=16,'row'=4,'col'=4] {'grp','row'}, dimensions={1}, use_global_device_ids=true | all-gather | bytes 99840 | tf_op jit(solution)/shard_map/all_gather | solution.py:83
  185.9 8.8 %all_gather.10 = f32[3,512]{1,0:T(4,128)S(1)} all-gather(f32[3,128]{1,0:T(4,128)} %param.12), channel_id=1, replica_groups=mesh['grp'=16,'row'=4,'col'=4] {'col'}, dimensions={1}, use_global_device_ids=true | all-gather | bytes 7680 | tf_op jit(solution)/shard_map/all_gather | solution.py:84
  194.7 2.3 copy.89
  197.0 2.3 copy.90
  199.2 2.9 fusion.7
  202.1 1.3 fusion.5
  205.7 9.1 %all_gather.11 = bf16[32,512]{0,1:T(8,128)(2,1)S(1)} all-gather(bf16[32,128]{0,1:T(8,128)(2,1)S(1)} %fusion.16), channel_id=1, replica_groups=mesh['grp'=16,'row'=4,'col'=4] {'col'}, dimensions={1}, use_global_device_ids=true | all-gather | bytes 40960 | tf_op jit(solution)/shard_map/all_gather | solution.py:85
  214.9 158.8 %while.13 = (s32[]{:T(128)}, f32[32,8192]{1,0:T(8,128)S(1)}, f32[3,8192]{1,0:T(4,128)}, f32[3,512]{1,0:T(4,128)S(1)}, s32[64,4]{0,1:T(4,128)S(1)}, /*index=5*/bf...) while((s32[]{:T(128)}, f32[32,8192]{1,0:T(8,128)S(1)}, ...), condition=%wide.region_1.2_spmd, body=%wide.region_0.1_spmd.sunk | while | flops 85524528 | bytes 11561869 | solution.py:111
  216.6 1.4 bitcast_divide_fusion.2
  218.0 8.4 %convolution_bitcast_fusion.5 = f32[32,1024]{1,0:T(8,128)S(1)} fusion(bf16[32,512]{1,0:T(8,128)(2,1)S(1)} %get-tuple-element.270, f32[1024,512]{1,0:T(8,128)S(1)} %bitcast_divide_fusion.2, f32[512]{0:T(512)S(1)} %bitcast.68, f32[1024]{0:T(1024)S(1)} %bitcast.62, f32[512]{0:T(512)S(1)} %bitcast.71, f32[1024]{0:T(1024)S(1)} %bitcast.59, ...), kind=kOutput, calls=%fused_computation.7.clone.1 | convolution fusion | flops 39845888 | bytes 2279424 | tf_op jit(solution)/shard_map/while/body/eval_jaxpr/dot_general | solution.py:101
  226.4 8.5 %convolution_bitcast_fusion.4 = f32[32,1024]{1,0:T(8,128)S(1)} fusion(bf16[32,512]{1,0:T(8,128)(2,1)S(1)} %get-tuple-element.270, f32[1024,512]{1,0:T(8,128)S(1)} %bitcast_divide_fusion.2, f32[512]{0:T(512)S(1)} %bitcast.69, f32[1024]{0:T(1024)S(1)} %bitcast.63, f32[512]{0:T(512)S(1)} %bitcast.72, f32[1024]{0:T(1024)S(1)} %bitcast.60, ...), kind=kOutput, calls=%fused_computation.6.clone.1 | convolution fusion | flops 39845888 | bytes 2279424 | tf_op jit(solution)/shard_map/while/body/eval_jaxpr/dot_general | solution.py:104
  235.0 0.9 constant_dynamic-slice_fusion.3
  236.4 1.4 bitcast_divide_fusion.2
  237.8 8.4 %convolution_bitcast_fusion.5 = f32[32,1024]{1,0:T(8,128)S(1)} fusion(bf16[32,512]{1,0:T(8,128)(2,1)S(1)} %get-tuple-element.270, f32[1024,512]{1,0:T(8,128)S(1)} %bitcast_divide_fusion.2, f32[512]{0:T(512)S(1)} %bitcast.68, f32[1024]{0:T(1024)S(1)} %bitcast.62, f32[512]{0:T(512)S(1)} %bitcast.71, f32[1024]{0:T(1024)S(1)} %bitcast.59, ...), kind=kOutput, calls=%fused_computation.7.clone.1 | convolution fusion | flops 39845888 | bytes 2279424 | tf_op jit(solution)/shard_map/while/body/eval_jaxpr/dot_general | solution.py:101
  246.2 8.5 %convolution_bitcast_fusion.4 = f32[32,1024]{1,0:T(8,128)S(1)} fusion(bf16[32,512]{1,0:T(8,128)(2,1)S(1)} %get-tuple-element.270, f32[1024,512]{1,0:T(8,128)S(1)} %bitcast_divide_fusion.2, f32[512]{0:T(512)S(1)} %bitcast.69, f32[1024]{0:T(1024)S(1)} %bitcast.63, f32[512]{0:T(512)S(1)} %bitcast.72, f32[1024]{0:T(1024)S(1)} %bitcast.60, ...), kind=kOutput, calls=%fused_computation.6.clone.1 | convolution fusion | flops 39845888 | bytes 2279424 | tf_op jit(solution)/shard_map/while/body/eval_jaxpr/dot_general | solution.py:104
  254.8 0.9 constant_dynamic-slice_fusion.3
  256.3 1.4 bitcast_divide_fusion.2
  257.6 8.4 %convolution_bitcast_fusion.5 = f32[32,1024]{1,0:T(8,128)S(1)} fusion(bf16[32,512]{1,0:T(8,128)(2,1)S(1)} %get-tuple-element.270, f32[1024,512]{1,0:T(8,128)S(1)} %bitcast_divide_fusion.2, f32[512]{0:T(512)S(1)} %bitcast.68, f32[1024]{0:T(1024)S(1)} %bitcast.62, f32[512]{0:T(512)S(1)} %bitcast.71, f32[1024]{0:T(1024)S(1)} %bitcast.59, ...), kind=kOutput, calls=%fused_computation.7.clone.1 | convolution fusion | flops 39845888 | bytes 2279424 | tf_op jit(solution)/shard_map/while/body/eval_jaxpr/dot_general | solution.py:101
  266.0 8.5 %convolution_bitcast_fusion.4 = f32[32,1024]{1,0:T(8,128)S(1)} fusion(bf16[32,512]{1,0:T(8,128)(2,1)S(1)} %get-tuple-element.270, f32[1024,512]{1,0:T(8,128)S(1)} %bitcast_divide_fusion.2, f32[512]{0:T(512)S(1)} %bitcast.69, f32[1024]{0:T(1024)S(1)} %bitcast.63, f32[512]{0:T(512)S(1)} %bitcast.72, f32[1024]{0:T(1024)S(1)} %bitcast.60, ...), kind=kOutput, calls=%fused_computation.6.clone.1 | convolution fusion | flops 39845888 | bytes 2279424 | tf_op jit(solution)/shard_map/while/body/eval_jaxpr/dot_general | solution.py:104
  276.1 1.4 bitcast_divide_fusion.2
  277.5 8.4 %convolution_bitcast_fusion.5 = f32[32,1024]{1,0:T(8,128)S(1)} fusion(bf16[32,512]{1,0:T(8,128)(2,1)S(1)} %get-tuple-element.270, f32[1024,512]{1,0:T(8,128)S(1)} %bitcast_divide_fusion.2, f32[512]{0:T(512)S(1)} %bitcast.68, f32[1024]{0:T(1024)S(1)} %bitcast.62, f32[512]{0:T(512)S(1)} %bitcast.71, f32[1024]{0:T(1024)S(1)} %bitcast.59, ...), kind=kOutput, calls=%fused_computation.7.clone.1 | convolution fusion | flops 39845888 | bytes 2279424 | tf_op jit(solution)/shard_map/while/body/eval_jaxpr/dot_general | solution.py:101
  285.9 8.5 %convolution_bitcast_fusion.4 = f32[32,1024]{1,0:T(8,128)S(1)} fusion(bf16[32,512]{1,0:T(8,128)(2,1)S(1)} %get-tuple-element.270, f32[1024,512]{1,0:T(8,128)S(1)} %bitcast_divide_fusion.2, f32[512]{0:T(512)S(1)} %bitcast.69, f32[1024]{0:T(1024)S(1)} %bitcast.63, f32[512]{0:T(512)S(1)} %bitcast.72, f32[1024]{0:T(1024)S(1)} %bitcast.60, ...), kind=kOutput, calls=%fused_computation.6.clone.1 | convolution fusion | flops 39845888 | bytes 2279424 | tf_op jit(solution)/shard_map/while/body/eval_jaxpr/dot_general | solution.py:104
  295.9 1.4 bitcast_divide_fusion.2
  297.3 8.4 %convolution_bitcast_fusion.5 = f32[32,1024]{1,0:T(8,128)S(1)} fusion(bf16[32,512]{1,0:T(8,128)(2,1)S(1)} %get-tuple-element.270, f32[1024,512]{1,0:T(8,128)S(1)} %bitcast_divide_fusion.2, f32[512]{0:T(512)S(1)} %bitcast.68, f32[1024]{0:T(1024)S(1)} %bitcast.62, f32[512]{0:T(512)S(1)} %bitcast.71, f32[1024]{0:T(1024)S(1)} %bitcast.59, ...), kind=kOutput, calls=%fused_computation.7.clone.1 | convolution fusion | flops 39845888 | bytes 2279424 | tf_op jit(solution)/shard_map/while/body/eval_jaxpr/dot_general | solution.py:101
  305.7 8.5 %convolution_bitcast_fusion.4 = f32[32,1024]{1,0:T(8,128)S(1)} fusion(bf16[32,512]{1,0:T(8,128)(2,1)S(1)} %get-tuple-element.270, f32[1024,512]{1,0:T(8,128)S(1)} %bitcast_divide_fusion.2, f32[512]{0:T(512)S(1)} %bitcast.69, f32[1024]{0:T(1024)S(1)} %bitcast.63, f32[512]{0:T(512)S(1)} %bitcast.72, f32[1024]{0:T(1024)S(1)} %bitcast.60, ...), kind=kOutput, calls=%fused_computation.6.clone.1 | convolution fusion | flops 39845888 | bytes 2279424 | tf_op jit(solution)/shard_map/while/body/eval_jaxpr/dot_general | solution.py:104
  315.7 1.4 bitcast_divide_fusion.2
  317.1 8.4 %convolution_bitcast_fusion.5 = f32[32,1024]{1,0:T(8,128)S(1)} fusion(bf16[32,512]{1,0:T(8,128)(2,1)S(1)} %get-tuple-element.270, f32[1024,512]{1,0:T(8,128)S(1)} %bitcast_divide_fusion.2, f32[512]{0:T(512)S(1)} %bitcast.68, f32[1024]{0:T(1024)S(1)} %bitcast.62, f32[512]{0:T(512)S(1)} %bitcast.71, f32[1024]{0:T(1024)S(1)} %bitcast.59, ...), kind=kOutput, calls=%fused_computation.7.clone.1 | convolution fusion | flops 39845888 | bytes 2279424 | tf_op jit(solution)/shard_map/while/body/eval_jaxpr/dot_general | solution.py:101
  325.5 8.5 %convolution_bitcast_fusion.4 = f32[32,1024]{1,0:T(8,128)S(1)} fusion(bf16[32,512]{1,0:T(8,128)(2,1)S(1)} %get-tuple-element.270, f32[1024,512]{1,0:T(8,128)S(1)} %bitcast_divide_fusion.2, f32[512]{0:T(512)S(1)} %bitcast.69, f32[1024]{0:T(1024)S(1)} %bitcast.63, f32[512]{0:T(512)S(1)} %bitcast.72, f32[1024]{0:T(1024)S(1)} %bitcast.60, ...), kind=kOutput, calls=%fused_computation.6.clone.1 | convolution fusion | flops 39845888 | bytes 2279424 | tf_op jit(solution)/shard_map/while/body/eval_jaxpr/dot_general | solution.py:104
  335.6 1.4 bitcast_divide_fusion.2
  336.9 8.4 %convolution_bitcast_fusion.5 = f32[32,1024]{1,0:T(8,128)S(1)} fusion(bf16[32,512]{1,0:T(8,128)(2,1)S(1)} %get-tuple-element.270, f32[1024,512]{1,0:T(8,128)S(1)} %bitcast_divide_fusion.2, f32[512]{0:T(512)S(1)} %bitcast.68, f32[1024]{0:T(1024)S(1)} %bitcast.62, f32[512]{0:T(512)S(1)} %bitcast.71, f32[1024]{0:T(1024)S(1)} %bitcast.59, ...), kind=kOutput, calls=%fused_computation.7.clone.1 | convolution fusion | flops 39845888 | bytes 2279424 | tf_op jit(solution)/shard_map/while/body/eval_jaxpr/dot_general | solution.py:101
  345.4 8.5 %convolution_bitcast_fusion.4 = f32[32,1024]{1,0:T(8,128)S(1)} fusion(bf16[32,512]{1,0:T(8,128)(2,1)S(1)} %get-tuple-element.270, f32[1024,512]{1,0:T(8,128)S(1)} %bitcast_divide_fusion.2, f32[512]{0:T(512)S(1)} %bitcast.69, f32[1024]{0:T(1024)S(1)} %bitcast.63, f32[512]{0:T(512)S(1)} %bitcast.72, f32[1024]{0:T(1024)S(1)} %bitcast.60, ...), kind=kOutput, calls=%fused_computation.6.clone.1 | convolution fusion | flops 39845888 | bytes 2279424 | tf_op jit(solution)/shard_map/while/body/eval_jaxpr/dot_general | solution.py:104
  355.4 1.4 bitcast_divide_fusion.2
  356.8 8.4 %convolution_bitcast_fusion.5 = f32[32,1024]{1,0:T(8,128)S(1)} fusion(bf16[32,512]{1,0:T(8,128)(2,1)S(1)} %get-tuple-element.270, f32[1024,512]{1,0:T(8,128)S(1)} %bitcast_divide_fusion.2, f32[512]{0:T(512)S(1)} %bitcast.68, f32[1024]{0:T(1024)S(1)} %bitcast.62, f32[512]{0:T(512)S(1)} %bitcast.71, f32[1024]{0:T(1024)S(1)} %bitcast.59, ...), kind=kOutput, calls=%fused_computation.7.clone.1 | convolution fusion | flops 39845888 | bytes 2279424 | tf_op jit(solution)/shard_map/while/body/eval_jaxpr/dot_general | solution.py:101
  365.2 8.5 %convolution_bitcast_fusion.4 = f32[32,1024]{1,0:T(8,128)S(1)} fusion(bf16[32,512]{1,0:T(8,128)(2,1)S(1)} %get-tuple-element.270, f32[1024,512]{1,0:T(8,128)S(1)} %bitcast_divide_fusion.2, f32[512]{0:T(512)S(1)} %bitcast.69, f32[1024]{0:T(1024)S(1)} %bitcast.63, f32[512]{0:T(512)S(1)} %bitcast.72, f32[1024]{0:T(1024)S(1)} %bitcast.60, ...), kind=kOutput, calls=%fused_computation.6.clone.1 | convolution fusion | flops 39845888 | bytes 2279424 | tf_op jit(solution)/shard_map/while/body/eval_jaxpr/dot_general | solution.py:104
  373.8 1.0 copy-done.1
  374.8 263.6 %reduce-scatter.2.cloned.1.call-done = f32[32,128]{1,0:T(8,128)} async-done(((f32[32,8192]{1,0:T(8,128)}), f32[32,128]{1,0:T(8,128)}) %reduce-scatter.2.cloned.1.call-update) | async-done | bytes 16400 | tf_op jit(solution)/shard_map/reduce_scatter | solution.py:114
  639.2 1.4 scatter_custom_fusion
  (111 shorter events, 20.4 us)
Async XLA Ops:
  7.2 631.2 %reduce-scatter.2.cloned.1.call-start = ((), (), s32[]{:S(2)}) async-start(), calls=%async_computation.1 | async-start | bytes 1064960 | tf_op jit(solution)/shard_map/reduce_scatter | solution.py:114
  8.2 22.6 %collective-permute-start.1 = (f32[32,1,8,128]{3,2,1,0:T(8,128)S(1)}, f32[32,1,8,128]{3,2,1,0:T(8,128)S(1)}, u32[]{:S(2)}, u32[]{:S(2)}) collective-permute-start(f32[32,1,8,128]{3,2,1,0:T(8,128)S(1)} %get-tuple-element.180), channel_id=1, source_target_pairs={{0,16},{16,32},{32,48},{48,64},{64,80},{80,96},{96,112},{112,128},... | collective-permute-start | bytes 393224 | tf_op jit(solution)/shard_map/ppermute | solution.py:28
  13.1 17.7 %collective-permute-start = (f32[32,1,8,128]{3,2,1,0:T(8,128)S(1)}, f32[32,1,8,128]{3,2,1,0:T(8,128)S(1)}, u32[]{:S(2)}, u32[]{:S(2)}) collective-permute-start(f32[32,1,8,128]{3,2,1,0:T(8,128)S(1)} %get-tuple-element.179), channel_id=1, source_target_pairs={{16,0},{32,16},{48,32},{64,48},{80,64},{96,80},{112,96},{128,112},... | collective-permute-start | bytes 393224 | tf_op jit(solution)/shard_map/ppermute | solution.py:29
  17.0 21.6 %copy-start.10 = (s32[128]{0:T(128)}, s32[128]{0:T(128)S(1)}, u32[]{:S(2)}) copy-start(s32[128]{0:T(128)S(1)} %compare_select_fusion) | copy-start | bytes 1540
  18.3 12.5 %copy-start = (f32[32,2,8,128]{3,2,1,0:T(8,128)S(1)}, f32[32,2,8,128]{3,2,1,0:T(8,128)}, u32[]{:S(2)}) copy-start(f32[32,2,8,128]{3,2,1,0:T(8,128)} %param.9) | copy-start | bytes 786436
  31.8 8.3 %collective-permute-start.2 = (f32[32,4,1,128]{3,0,2,1:T(8,128)S(1)}, f32[32,4,1,128]{3,0,2,1:T(8,128)S(1)}, u32[]{:S(2)}, u32[]{:S(2)}) collective-permute-start(f32[32,4,1,128]{3,0,2,1:T(8,128)S(1)} %copy.91), channel_id=1, source_target_pairs={{4,0},{8,4},{12,8},{5,1},{9,5},{13,9},{6,2},{10,6},{14,10},{7,3},{... | collective-permute-start | bytes 196616 | tf_op jit(solution)/shard_map/ppermute | solution.py:29
  33.1 7.1 %collective-permute-start.3 = (f32[32,4,1,128]{3,0,2,1:T(8,128)S(1)}, f32[32,4,1,128]{3,0,2,1:T(8,128)S(1)}, u32[]{:S(2)}, u32[]{:S(2)}) collective-permute-start(f32[32,4,1,128]{3,0,2,1:T(8,128)S(1)} %copy.92), channel_id=1, source_target_pairs={{0,4},{4,8},{8,12},{1,5},{5,9},{9,13},{2,6},{6,10},{10,14},{3,7},{... | collective-permute-start | bytes 196616 | tf_op jit(solution)/shard_map/ppermute | solution.py:28
  40.0 7.0 %copy-start.7 = (f32[3,128]{1,0:T(4,128)S(1)}, f32[3,128]{1,0:T(4,128)}, u32[]{:S(2)}) copy-start(f32[3,128]{1,0:T(4,128)} %param.12) | copy-start | bytes 4612
  40.2 6.8 %copy-start.2 = (f32[32,4,1,128]{0,2,3,1:T(1,128)}, f32[32,4,1,128]{0,2,3,1:T(1,128)S(1)}, u32[]{:S(2)}) copy-start(f32[32,4,1,128]{0,2,3,1:T(1,128)S(1)} %copy.71) | copy-start | bytes 196612
  40.3 6.6 %copy-start.3 = (f32[32,4,1,128]{0,2,3,1:T(1,128)}, f32[32,4,1,128]{0,2,3,1:T(1,128)S(1)}, u32[]{:S(2)}) copy-start(f32[32,4,1,128]{0,2,3,1:T(1,128)S(1)} %copy.73) | copy-start | bytes 196612
  41.1 158.1 %collective-permute-start.4 = (f32[32,4,10,1]{0,2,3,1:T(8,128)}, f32[32,4,10,1]{0,2,3,1:T(8,128)}, u32[]{:S(2)}, u32[]{:S(2)}) collective-permute-start(f32[32,4,10,1]{0,2,3,1:T(8,128)} %get-tuple-element.170), channel_id=1, source_target_pairs={{1,0},{2,1},{3,2},{5,4},{6,5},{7,6},{9,8},{10,9},{11,10},{13,12},{... | collective-permute-start | bytes 15368 | tf_op jit(solution)/shard_map/ppermute | solution.py:29
  42.4 156.8 %collective-permute-start.5 = (f32[32,4,10,1]{0,2,3,1:T(8,128)}, f32[32,4,10,1]{0,2,3,1:T(8,128)}, u32[]{:S(2)}, u32[]{:S(2)}) collective-permute-start(f32[32,4,10,1]{0,2,3,1:T(8,128)} %get-tuple-element.171), channel_id=1, source_target_pairs={{0,1},{1,2},{2,3},{4,5},{5,6},{6,7},{8,9},{9,10},{10,11},{12,13},{... | collective-permute-start | bytes 15368 | tf_op jit(solution)/shard_map/ppermute | solution.py:28
  199.2 2.9 copy-start.4
  203.4 1.0 copy-start.5
  203.4 0.9 copy-start.6
  203.8 1.8 copy-start.8
  203.8 1.8 copy-start.9
  373.8 1.0 copy-start.1
Sparse Core Ops, SparseCore 0:
  374.9 263.4 reduce-scatter.1
where the time goes:
time: 651 us; the launch traced here: 649 us
  waiting for transfers between devices  264 us (41%)
  blocking collectives  155 us (24%)
  matrix products  135 us (21%)
  local copies, waits for them, and re-layouts  36.5 us (6%)
  other arithmetic  23.8 us (4%)
  starting transfers between devices  19.6 us (3%)
  between operations  14.4 us (2%)
    reduce_scatter x1, waiting for transfers between devices, on_device(): lax.psum_scatter(partial_value, ('grp', 'row'), scatter_dimension=1, tile...  264 us
    all_gather x1, blocking collectives, on_device(): targets = lax.all_gather(points, ('grp', 'row'), axis=1, tiled=True)  137 us
    dot_general x8, matrix products, one_block(): lax.dot_general(source_traces, tile_imag, CONTRACT, preferred_element_typ...  68.1 us
    dot_general x8, matrix products, one_block(): lax.dot_general(source_traces, tile_real, CONTRACT, preferred_element_typ...  67.3 us
    ppermute x3, starting transfers between devices, padded_2(): before = lax.ppermute(last, axis, up)  15.1 us
  transfers between devices with their start and end apart: 7, of which 1 were waited for; matrix products, arithmetic and copies ran while one was open for 4% of the time, Pallas kernels for 0%

commit v1 on v0

v1 whole, which is shorter than its diff:
```python
import math

import jax
import jax.numpy as jnp
import numpy as np
from jax import lax
from jax.experimental import pallas as pl
from jax.experimental.pallas import tpu as pltpu
from jax.sharding import Mesh
from jax.sharding import PartitionSpec as P

RHS = 16
CX = 2
CY = 8
CZ = 128
CH = 32
PTS = 128

FOUR_PI = 4.0 * 3.141592653589793
WAVENUMBER = 10.0
SOFTENING = 0.01
RELAX_RATE = 0.8
COUPLING = 0.5

TURN = WAVENUMBER / (2.0 * 3.141592653589793)
CENTRE = 2.0
SCALE = TURN / FOUR_PI

ALPHA = ("zl", "core", "zh")
BETA = ("x", "y")
SIDE = 16
EXT = 32
NT = 4
LIST = 256 + 4 * NT

f32, bf16, i32 = jnp.float32, jnp.bfloat16, jnp.int32


def sine_coefficients():
    f = np.cos(np.linspace(0, np.pi / 2, 4001)) * 0.5 + 1e-9
    z = f * f
    y = np.sin(np.pi / 2 * f) / f
    basis = np.stack([np.ones_like(z), z, z * z], 1)
    weight = np.ones_like(f)
    fit = None
    for _ in range(300):
        fit, *_ = np.linalg.lstsq(basis * (weight * f)[:, None], y * weight * f, rcond=None)
        err = np.abs((basis @ fit - y) * f)
        weight = weight * (1e-12 + err / err.max()) ** 0.3
        weight = weight / weight.max()
    return [float(c) for c in fit]


SIN = sine_coefficients()
LAM2 = 2.0 * math.sqrt(2.0)
LAM = math.sqrt(LAM2)
RT2 = math.sqrt(2.0)
S0, S1, S2 = [c * LAM for c in SIN]


def dot(a, b, dims):
    return lax.dot_general(a, b, (dims, ((), ())), preferred_element_type=f32)


def split3(x):
    hi = x.astype(bf16).astype(f32)
    rest = x - hi
    mid = rest.astype(bf16).astype(f32)
    return hi, mid, rest - mid


def ext_kernel(where_ref, pts_ref, near_ref, src_ref, tgt_ref, flags_ref, scr):
    p = (pts_ref[...] - CENTRE) * TURN
    r = jnp.sum(p * p, axis=0, keepdims=True)
    ah, am, al = split3(-2.0 * p)
    bh, bm, bl = split3(p)
    sh, sm, sl = split3(r)
    th, tm, tl = split3(r + SOFTENING * TURN * TURN)
    one = jnp.ones((1, PTS), f32)
    for out, groups in (
        (src_ref, ((ah, sh), (ah, one), (am, sm), (am, one), (ah, sl), (al, one))),
        (tgt_ref, ((bh, one), (bm, th), (bh, one), (bm, tm), (bl, one), (bh, tl))),
    ):
        scr[...] = jnp.zeros((EXT, PTS), f32)
        for n, (three, last) in enumerate(groups):
            scr[4 * n : 4 * n + 3, :] = three
            scr[4 * n + 3 : 4 * n + 4, :] = last
        out[...] = scr[...].astype(bf16)
    base_row = where_ref[0]
    base_col = where_ref[1]
    rows = lax.broadcasted_iota(i32, (SIDE, 256), 0)
    cols = lax.broadcasted_iota(i32, (SIDE, 256), 1)
    pick_rows = (cols == rows * 4 + base_row).astype(f32).astype(bf16)
    rows = lax.broadcasted_iota(i32, (256, PTS), 0)
    cols = lax.broadcasted_iota(i32, (256, PTS), 1)
    pick_cols = ((rows == (cols // 4) * 64 + cols % 4 + base_col) & (cols < SIDE)).astype(f32).astype(bf16)
    near = (near_ref[...] != 0).astype(f32).astype(bf16)
    some = dot(pick_rows, near, ((1,), (0,))).astype(bf16)
    flags_ref[...] = dot(some, pick_cols, ((1,), (0,))).astype(i32)


def list_kernel(flags_ref, list_ref, count_ref):
    def clear(k, _):
        list_ref[k] = SIDE
        return 0

    lax.fori_loop(0, LIST, clear, 0)

    def one(k, n):
        i = k // SIDE
        j = k % SIDE
        list_ref[n] = jnp.where(flags_ref[i, j] != 0, i * 32 + j, SIDE)
        return n + flags_ref[i, j]

    count_ref[0] = lax.fori_loop(0, SIDE * SIDE, one, jnp.int32(0))


def faces_kernel(vol_ref, xu_ref, xd_ref, yu_ref, yd_ref, zu_ref, zd_ref):
    xu_ref[...] = vol_ref[:, CX - 1].astype(bf16)
    xd_ref[...] = vol_ref[:, 0].astype(bf16)
    yu_ref[...] = vol_ref[:, :, CY - 1, :].reshape(CH * CX, CZ).astype(bf16)
    yd_ref[...] = vol_ref[:, :, 0, :].reshape(CH * CX, CZ).astype(bf16)
    v = vol_ref[...].reshape(CH * CX * CY, CZ).astype(bf16)
    rows = lax.broadcasted_iota(i32, (16, CZ), 0)
    cols = lax.broadcasted_iota(i32, (16, CZ), 1)
    up = ((rows == 0) & (cols == CZ - 1)).astype(f32).astype(bf16)
    down = ((rows == 1) & (cols == 0)).astype(f32).astype(bf16)
    zu_ref[...] = dot(up, v, ((1,), (1,))).astype(bf16)
    zd_ref[...] = dot(down, v, ((1,), (1,))).astype(bf16)


def relax_kernel(vol_ref, forc_ref, med_ref, xl_ref, xh_ref, yl_ref, yh_ref, zl_ref, zh_ref,
                 wts_ref, map_ref, rel_ref, tr_ref):
    v = vol_ref[...]
    xl = xl_ref[...].astype(f32)
    xh = xh_ref[...].astype(f32)
    bx = jnp.stack([xl + v[:, 1], v[:, 0] + xh], axis=1)
    v3 = v.reshape(CH * CX, CY, CZ)
    row = lax.broadcasted_iota(i32, v3.shape, 1)
    yl = yl_ref[...].astype(f32)[:, None, :]
    yh = yh_ref[...].astype(f32)[:, None, :]
    by = jnp.where(row == 0, yl, pltpu.roll(v3, 1, 1)) + jnp.where(row == CY - 1, yh, pltpu.roll(v3, CY - 1, 1))
    v2 = v.reshape(CH * CX * CY, CZ)
    lane = lax.broadcasted_iota(i32, v2.shape, 1)
    rows = lax.broadcasted_iota(i32, (16, CZ), 0)
    cols = lax.broadcasted_iota(i32, (16, CZ), 1)
    place = (((rows == 0) & (cols == 0)) | ((rows == 1) & (cols == CZ - 1))).astype(f32).astype(bf16)
    zhalo = (zl_ref[...].astype(f32) + zh_ref[...].astype(f32)).astype(bf16)
    bz = (
        jnp.where(lane == 0, 0.0, pltpu.roll(v2, 1, 1))
        + jnp.where(lane == CZ - 1, 0.0, pltpu.roll(v2, CZ - 1, 1))
        + dot(zhalo, place, ((0,), (0,)))
    )
    beside = bx + by.reshape(v.shape) + bz.reshape(v.shape)
    a = med_ref[0]
    b = med_ref[1]
    lap = 6.0 * v - beside
    re, im = v[:RHS], v[RHS:]
    out_re = lap[:RHS] - a[None] * re + b[None] * im
    out_im = lap[RHS:] - a[None] * im - b[None] * re
    res = forc_ref[...] - jnp.concatenate([out_re, out_im], 0)
    rate = RELAX_RATE / (6.0 - a)
    relaxed = v + res * rate[None]
    rel_ref[...] = relaxed
    cells = map_ref[...]
    sub = lax.broadcasted_iota(i32, (CZ, PTS), 0)
    pick = (sub == cells % CZ).astype(f32).astype(bf16)
    hi, mid, lo = split3(relaxed.reshape(CH * CX * CY, CZ))
    at = (
        dot(hi.astype(bf16), pick, ((1,), (0,)))
        + dot(mid.astype(bf16), pick, ((1,), (0,)))
        + dot(lo.astype(bf16), pick, ((1,), (0,)))
    )
    rid = lax.broadcasted_iota(i32, (CX * CY, PTS), 0)
    keep = (rid == cells // CZ).astype(f32)
    at = at.reshape(CH, CX * CY, PTS) * keep[None]
    tr_ref[...] = (jnp.sum(at, axis=1) * wts_ref[...]).astype(bf16)


def evaluate(dist2):
    inv = lax.rsqrt(dist2)
    turns = dist2 * inv
    f = turns - jnp.round(turns)
    z = f * f
    s = f * ((S2 * z + S1) * z + S0)
    a = s * s
    c2 = RT2 - a
    w = LAM2 - a
    c = w * lax.rsqrt(w)
    s2 = s * c
    e = s2 * inv
    return (inv - e * s2).astype(bf16), (e * c2).astype(bf16)


def pair_kernel(list_ref, count_ref, src_ref, tgt_ref, tr_ref, out_ref, a_ref, w_ref, d0, d1, g0, g1):
    out_ref[...] = jnp.zeros_like(out_ref)
    for j in range(SIDE):
        a_ref[j] = jnp.transpose(src_ref[j].astype(f32)).astype(bf16)
        t = tr_ref[j]
        w_ref[j, :, 0:PTS] = t
        w_ref[j, :, PTS:] = jnp.concatenate([-t[RHS:], t[:RHS]], 0)
    a_ref[SIDE] = a_ref[0]
    w_ref[SIDE] = jnp.zeros((CH, 2 * PTS), bf16)
    pairs = (count_ref[0] + (2 * NT - 1)) // (2 * NT)

    def code(group, q):
        c = list_ref[group * NT + q]
        return c // 32, c % 32

    def dist(group, d_ref):
        for q in range(NT):
            i, j = code(group, q)
            d_ref[q] = jnp.dot(a_ref[j], tgt_ref[i], preferred_element_type=f32)

    def add(group, g_ref):
        for q in range(NT):
            i, j = code(group, q)
            out_ref[i] += jnp.dot(w_ref[j], g_ref[q], preferred_element_type=f32)

    def values(d_ref, g_ref):
        for q in range(NT):
            re, im = evaluate(d_ref[q])
            g_ref[q, 0:PTS, :] = re
            g_ref[q, PTS:, :] = im

    dist(0, d0)
    g1[...] = jnp.zeros_like(g1)

    def body(k, _):
        dist(2 * k + 1, d1)
        values(d0, g0)
        add(jnp.maximum(2 * k - 1, 0), g1)
        dist(2 * k + 2, d0)
        values(d1, g1)
        add(2 * k, g0)
        return 0

    lax.fori_loop(0, pairs, body, 0)
    add(jnp.maximum(2 * pairs - 1, 0), g1)


def finish_kernel(part_ref, rel_ref, map_ref, new_ref, pot_ref):
    pot = jnp.sum(part_ref[...].astype(f32), axis=0) * SCALE
    pot_ref[...] = pot
    cells = map_ref[...]
    rid = lax.broadcasted_iota(i32, (CX * CY, PTS), 0)
    keep = (rid == cells // CZ).astype(f32)
    sub = lax.broadcasted_iota(i32, (CZ, PTS), 0)
    pick = (sub == cells % CZ).astype(f32).astype(bf16)
    spread = jnp.zeros((CH * CX * CY, CZ), f32)
    for part in split3(pot * COUPLING):
        wide = (part[:, None, :] * keep[None]).reshape(CH * CX * CY, PTS).astype(bf16)
        spread = spread + dot(wide, pick, ((1,), (1,)))
    new_ref[...] = rel_ref[...] + spread.reshape(CH, CX, CY, CZ)


def vmem(n):
    return [pl.BlockSpec(memory_space=pltpu.VMEM)] * n


def smem(n):
    return [pl.BlockSpec(memory_space=pltpu.SMEM)] * n


def shaped(*shapes):
    return [jax.ShapeDtypeStruct(s, d) for s, d in shapes]


def step(x, axes, delta):
    size = 1
    for axis in axes:
        size *= lax.axis_size(axis)
    pairs = [(k, k + delta) for k in range(size) if 0 <= k + delta < size]
    return lax.ppermute(x, axes if len(axes) > 1 else axes[0], pairs)


def everyone(x, axes):
    return lax.all_to_all(jnp.broadcast_to(x[None], (SIDE,) + x.shape), axes, 0, 0, tiled=True)


def on_device(volume, forcing, medium, points, weights, cell_map, near_list):
    cells = cell_map[None, :]
    wts = weights[None, :]
    ax, ay = lax.axis_index("x"), lax.axis_index("y")
    alpha = lax.axis_index(ALPHA)
    where = jnp.stack([ax * 64 + ay, alpha * 4]).astype(i32)
    src, tgt, flags = pl.pallas_call(
        ext_kernel,
        out_shape=shaped(((EXT, PTS), bf16), ((EXT, PTS), bf16), ((SIDE, PTS), i32)),
        in_specs=smem(1) + vmem(2),
        out_specs=vmem(3),
        scratch_shapes=[pltpu.VMEM((EXT, PTS), f32)],
        name="ext",
    )(where, points, near_list)
    targets = everyone(tgt, ALPHA)
    sources = everyone(src, BETA)
    xu, xd, yu, yd, zu, zd = pl.pallas_call(
        faces_kernel,
        out_shape=shaped(
            *[((CH, CY, CZ), bf16)] * 2, *[((CH * CX, CZ), bf16)] * 2, *[((16, CH * CX * CY), bf16)] * 2
        ),
        in_specs=vmem(1),
        out_specs=vmem(6),
        name="faces",
    )(volume)
    grp = ("x", "zl", "core")
    xl, xh = step(xu, grp, 1), step(xd, grp, -1)
    yl, yh = step(yu, ("zh",), 1), step(yd, ("zh",), -1)
    zl, zh = step(zu, ("y",), 1), step(zd, ("y",), -1)
    order, count = pl.pallas_call(
        list_kernel,
        out_shape=shaped(((LIST,), i32), ((1,), i32)),
        in_specs=smem(1),
        out_specs=smem(2),
        name="order",
    )(flags)
    relaxed, traces = pl.pallas_call(
        relax_kernel,
        out_shape=shaped(((CH, CX, CY, CZ), f32), ((CH, PTS), bf16)),
        in_specs=vmem(11),
        out_specs=vmem(2),
        name="relax",
    )(volume, forcing, medium, xl, xh, yl, yh, zl, zh, wts, cells)
    source_traces = everyone(traces, BETA)
    part = pl.pallas_call(
        pair_kernel,
        out_shape=jax.ShapeDtypeStruct((SIDE, CH, PTS), f32),
        in_specs=smem(2) + vmem(3),
        out_specs=vmem(1)[0],
        scratch_shapes=[
            pltpu.VMEM((SIDE + 1, PTS, EXT), bf16),
            pltpu.VMEM((SIDE + 1, CH, 2 * PTS), bf16),
            pltpu.VMEM((NT, PTS, PTS), f32),
            pltpu.VMEM((NT, PTS, PTS), f32),
            pltpu.VMEM((NT, 2 * PTS, PTS), bf16),
            pltpu.VMEM((NT, 2 * PTS, PTS), bf16),
        ],
        name="pairs",
    )(order, count, sources, targets, source_traces)
    parts = lax.all_to_all(part, ALPHA, 0, 0, tiled=True)
    new_volume, potential = pl.pallas_call(
        finish_kernel,
        out_shape=shaped(((CH, CX, CY, CZ), f32), ((CH, PTS), f32)),
        in_specs=vmem(3),
        out_specs=vmem(2),
        name="finish",
    )(parts, relaxed, cells)
    return new_volume, potential


def solution(mesh):
    split = Mesh(np.asarray(mesh.devices).reshape(4, 2, 2, 4, 4), ("x", "zl", "core", "zh", "y"))
    grid = P(None, ("x", "zl", "core"), "zh", "y")
    all_axes = ("x", "zl", "core", "zh", "y")
    return jax.shard_map(
        on_device,
        mesh=split,
        in_specs=(grid, grid, grid, P(None, all_axes), P(all_axes), P(all_axes), P()),
        out_specs=(grid, P(None, all_axes)),
        check_vma=False,
    )
```

time: 651 us -> 108 us (0.17)
  waiting for transfers between devices: 264 us -> 5.88 us
  matrix products: 135 us -> 0 us
  blocking collectives: 155 us -> 30 us
  local copies, waits for them, and re-layouts: 36.5 us -> 4.03 us
  Pallas kernels: 0 us -> 27.5 us
  other arithmetic: 23.8 us -> 0.62 us
  starting transfers between devices: 19.6 us -> 38.8 us
  between operations: 14.4 us -> 0.78 us
    reduce_scatter x1 -> x0, waiting for transfers between devices: 264 us -> none  [on_device(): lax.psum_scatter(partial_value, ('grp', 'row'), scatter_dimension=1, tile...]
    all_gather x3 -> x0, blocking collectives: 155 us -> none  [the longest x1 137 us: on_device(): targets = lax.all_gather(points, ('grp', 'row'), axis=1, tiled=True)]
    dot_general x16 -> x0, matrix products: 135 us -> none  [the longest x8 68.1 us: one_block(): lax.dot_general(source_traces, tile_imag, CONTRACT, preferred_element_typ...]
    all_to_all x0 -> x2, blocking collectives: none -> 30 us  [the longest x1 17 us: on_device(): parts = lax.all_to_all(part, ALPHA, 0, 0, tiled=True)]
    pallas_call x0 -> x6, Pallas kernels: none -> 27.5 us  [the longest x1 13.1 us: on_device(): pl.pallas_call(pair_kernel, out_shape=jax.ShapeDtypeStruct((SIDE, CH, PTS...]
    all_to_all x0 -> x2, starting transfers between devices: none -> 21.5 us  [everyone(): lax.all_to_all(jnp.broadcast_to(x[None], (SIDE,) + x.shape), axes, 0, 0,...]
    div x9 -> x0, other arithmetic: 12.4 us -> none  [the longest x8 11 us: kernel_tiles(): factor = listed / (FOUR_PI * distance)]
    reshape x1 -> x0, local copies, waits for them, and re-layouts: 10.9 us -> none  [on_device(): near_list.reshape(group_count, column_count, group_count, column_count)]
  transfers between devices with their start and end apart: 7 -> 8, of which waited for: 1 -> 3; matrix products, arithmetic and copies ran while one was open for 4% -> 0% of each run, Pallas kernels for 0% -> 10%
where the time goes in v1:
time: 108 us
  starting transfers between devices  38.8 us (36%)
  blocking collectives  30 us (28%)
  Pallas kernels  27.5 us (25%)
  waiting for transfers between devices  5.88 us (5%)
  local copies, waits for them, and re-layouts  4.03 us (4%)
    all_to_all x2, starting transfers between devices, everyone(): lax.all_to_all(jnp.broadcast_to(x[None], (SIDE,) + x.shape), axes, 0, 0,...  21.5 us
    ppermute x6, starting transfers between devices, step(): return lax.ppermute(x, axes if len(axes) > 1 else axes[0], pairs)  17.3 us
    all_to_all x1, blocking collectives, on_device(): parts = lax.all_to_all(part, ALPHA, 0, 0, tiled=True)  17 us
    pallas_call x1, Pallas kernels, on_device(): pl.pallas_call(pair_kernel, out_shape=jax.ShapeDtypeStruct((SIDE, CH, PTS...  13.1 us
    all_to_all x1, blocking collectives, everyone(): lax.all_to_all(jnp.broadcast_to(x[None], (SIDE,) + x.shape), axes, 0, 0,...  13.1 us
    pallas_call x1, Pallas kernels, on_device(): pl.pallas_call(list_kernel, out_shape=shaped(((LIST,), i32), ((1,), i32))...  6.44 us
    ppermute x6, waiting for transfers between devices, step(): return lax.ppermute(x, axes if len(axes) > 1 else axes[0], pairs)  3.4 us
    broadcast_in_dim x3, local copies, waits for them, and re-layouts, everyone(): jnp.broadcast_to(x[None], (SIDE,) + x.shape)  2.76 us
  transfers between devices with their start and end apart: 8, of which 3 were waited for; matrix products, arithmetic and copies ran while one was open for 0% of the time, Pallas kernels for 10%

profile of v1, /device:TPU:1, one launch (start us, length us, event | category | flops | bytes accessed | tf_op | source)
XLA Modules:
  0.0 107.6 jit_solution(15253134663356829187)
XLA Ops:
  0.6 0.6 pad_add_fusion.where_ref
  1.3 1.8 %ext.1 = (bf16[32,128]{1,0:T(8,128)(2,1)}, bf16[32,128]{1,0:T(8,128)(2,1)}, s32[16,128]{1,0:T(8,128)}) custom-call(s32[2]{0:T(128)} %pad_add_fusion.where_ref, f32[3,128]{1,0:T(4,128)} %pts_ref.1, s32[256,256]{1,0:T(8,128)} %near_ref.1), custom_call_target="tpu_custom_call" | custom-call | tf_op jit(solution)/shard_map/ext/pallas_call | solution.py:287
  3.1 1.4 %broadcast_in_dim.10 = bf16[16,32,128]{2,1,0:T(8,128)(2,1)} broadcast(bf16[32,128]{1,0:T(8,128)(2,1)} %get-tuple-element.18), dimensions={1,2} | broadcast | bytes 139264 | tf_op jit(solution)/shard_map/broadcast_in_dim | solution.py:278
  4.5 7.6 %all-to-all-start = ((bf16[16,32,128]{2,1,0:T(8,128)(2,1)}), bf16[16,32,128]{2,1,0:T(8,128)(2,1)S(1)}, u32[]{:S(2)}, u32[]{:S(2)}) async-start(bf16[16,32,128]{2,1,0:T(8,128)(2,1)} %broadcast_in_dim.10), calls=%async_computation | async-start | bytes 262144 | tf_op jit(solution)/shard_map/all_to_all | solution.py:278
  12.0 1.7 %faces.1 = (bf16[32,8,128]{2,1,0:T(8,128)(2,1)}, bf16[32,8,128]{2,1,0:T(8,128)(2,1)}, bf16[64,128]{1,0:T(8,128)(2,1)}, bf16[64,128]{1,0:T(8,128)(2,1)}, bf16[16,...) custom-call(f32[32,2,8,128]{3,2,1,0:T(8,128)} %vol_ref.3), custom_call_target="tpu_custom_call" | custom-call | tf_op jit(solution)/shard_map/faces/pallas_call | solution.py:297
  13.8 4.4 %collective-permute-start = (bf16[32,8,128]{2,1,0:T(8,128)(2,1)}, bf16[32,8,128]{2,1,0:T(8,128)(2,1)S(1)}, u32[]{:S(2)}, u32[]{:S(2)}) collective-permute-start(bf16[32,8,128]{2,1,0:T(8,128)(2,1)} %get-tuple-element.20), channel_id=1, source_target_pairs={{0,16},{16,32},{32,48},{48,64},{64,80},{80,96},{96,112},{112,128},... | collective-permute-start | bytes 196616 | tf_op jit(solution)/shard_map/ppermute | solution.py:274
  18.2 1.9 %collective-permute-start.1 = (bf16[32,8,128]{2,1,0:T(8,128)(2,1)}, bf16[32,8,128]{2,1,0:T(8,128)(2,1)S(1)}, u32[]{:S(2)}, u32[]{:S(2)}) collective-permute-start(bf16[32,8,128]{2,1,0:T(8,128)(2,1)} %get-tuple-element.21), channel_id=1, source_target_pairs={{16,0},{32,16},{48,32},{64,48},{80,64},{96,80},{112,96},{128,112},... | collective-permute-start | bytes 196616 | tf_op jit(solution)/shard_map/ppermute | solution.py:274
  20.1 4.9 %collective-permute-start.2 = (bf16[64,128]{1,0:T(8,128)(2,1)}, bf16[64,128]{1,0:T(8,128)(2,1)S(1)}, u32[]{:S(2)}, u32[]{:S(2)}) collective-permute-start(bf16[64,128]{1,0:T(8,128)(2,1)} %get-tuple-element.22), channel_id=1, source_target_pairs={{0,4},{4,8},{8,12},{1,5},{5,9},{9,13},{2,6},{6,10},{10,14},{3,7},{... | collective-permute-start | bytes 49160 | tf_op jit(solution)/shard_map/ppermute | solution.py:274
  25.0 1.3 %collective-permute-start.3 = (bf16[64,128]{1,0:T(8,128)(2,1)}, bf16[64,128]{1,0:T(8,128)(2,1)S(1)}, u32[]{:S(2)}, u32[]{:S(2)}) collective-permute-start(bf16[64,128]{1,0:T(8,128)(2,1)} %get-tuple-element.23), channel_id=1, source_target_pairs={{4,0},{8,4},{12,8},{5,1},{9,5},{13,9},{6,2},{10,6},{14,10},{7,3},{... | collective-permute-start | bytes 49160 | tf_op jit(solution)/shard_map/ppermute | solution.py:274
  26.3 3.5 %collective-permute-start.4 = (bf16[16,512]{1,0:T(8,128)(2,1)}, bf16[16,512]{1,0:T(8,128)(2,1)S(1)}, u32[]{:S(2)}, u32[]{:S(2)}) collective-permute-start(bf16[16,512]{1,0:T(8,128)(2,1)} %get-tuple-element.24), channel_id=1, source_target_pairs={{0,1},{1,2},{2,3},{4,5},{5,6},{6,7},{8,9},{9,10},{10,11},{12,13},{... | collective-permute-start | bytes 49160 | tf_op jit(solution)/shard_map/ppermute | solution.py:274
  29.9 0.0 collective-permute-done.2.yl_ref
  29.9 0.0 copy-start.4
  29.9 1.3 %collective-permute-start.5 = (bf16[16,512]{1,0:T(8,128)(2,1)}, bf16[16,512]{1,0:T(8,128)(2,1)S(1)}, u32[]{:S(2)}, u32[]{:S(2)}) collective-permute-start(bf16[16,512]{1,0:T(8,128)(2,1)} %get-tuple-element.25), channel_id=1, source_target_pairs={{1,0},{2,1},{3,2},{5,4},{6,5},{7,6},{9,8},{10,9},{11,10},{13,12},{... | collective-permute-start | bytes 49160 | tf_op jit(solution)/shard_map/ppermute | solution.py:274
  31.2 0.4 collective-permute-done.3.yh_ref
  31.6 0.0 copy-start.5
  31.6 0.0 collective-permute-done.4.zl_ref
  31.6 0.0 copy-start.6
  31.6 3.0 %collective-permute-done.5.zh_ref = bf16[16,512]{1,0:T(8,128)(2,1)S(1)} collective-permute-done((bf16[16,512]{1,0:T(8,128)(2,1)}, bf16[16,512]{1,0:T(8,128)(2,1)S(1)}, u32[]{:S(2)}, u32[]{:S(2)}) %collective-permute-start.5) | collective-permute-done | bytes 16416 | tf_op jit(solution)/shard_map/ppermute | solution.py:274
  34.6 0.0 copy-start.7
  34.6 0.0 collective-permute-done.xl_ref
  34.6 0.0 copy-start.2
  34.6 0.0 collective-permute-done.1.xh_ref
  34.6 0.0 copy-start.3
  34.6 0.0 copy-done.4
  34.6 0.0 copy-done.5
  34.6 0.0 copy-done.6
  34.6 0.5 copy-done.7
  35.2 0.0 copy-done.2
  35.2 0.0 copy-done.3
  35.2 2.3 %relax.1 = (f32[32,2,8,128]{3,2,1,0:T(8,128)}, bf16[32,128]{1,0:T(8,128)(2,1)}) custom-call(f32[32,2,8,128]{3,2,1,0:T(8,128)} %vol_ref.3, f32[32,2,8,128]{3,2,1,0:T(8,128)} %forc_ref.1, f32[2,2,8,128]{3,2,1,0:T(8,128)} %med_ref.1, bf16[32,8,128]{2,1,0:T(8,128)(2,1)} %copy-done.2, bf16[32,8,128]{2,1,0:T(8,128)(2,1)} %copy-done.3, bf16[64,128]{1,0:T(8,128)(2,1)} %copy-done.4, ...), custom_call_target="tpu_custom_call" | custom-call | tf_op jit(solution)/shard_map/relax/pallas_call | solution.py:317
  37.5 0.0 all-to-all-done.src_ref
  37.5 0.0 copy-start
  37.5 0.7 broadcast_in_dim.28
  38.3 0.0 copy-start.8
  38.3 13.1 %all_to_all.20.tr_ref = bf16[16,32,128]{2,1,0:T(8,128)(2,1)} all-to-all(bf16[16,32,128]{2,1,0:T(8,128)(2,1)S(1)} %broadcast_in_dim.28), channel_id=1, replica_groups=mesh['x'=4,'zl'=2,'core'=2,'zh'=4,'y'=4] {'x','y'}, dimensions={0} | all-to-all | bytes 262144 | tf_op jit(solution)/shard_map/all_to_all | solution.py:278
  51.4 0.0 copy-done
  51.4 0.0 copy-done.8
  51.4 0.7 broadcast_in_dim.11
  52.0 13.9 %all-to-all-start.1 = ((bf16[16,32,128]{2,1,0:T(8,128)(2,1)}), bf16[16,32,128]{2,1,0:T(8,128)(2,1)S(1)}, u32[]{:S(2)}, u32[]{:S(2)}) async-start(bf16[16,32,128]{2,1,0:T(8,128)(2,1)} %broadcast_in_dim.11), calls=%async_computation.1 | async-start | bytes 262144 | tf_op jit(solution)/shard_map/all_to_all | solution.py:278
  65.9 6.4 %order.1 = (s32[272]{0:T(512)}, s32[1]{0:T(128)}) custom-call(s32[16,128]{1,0:T(8,128)} %get-tuple-element.15.flags_ref), custom_call_target="tpu_custom_call" | custom-call | tf_op jit(solution)/shard_map/order/pallas_call | solution.py:310
  72.4 2.5 %all-to-all-done.1.tgt_ref = bf16[16,32,128]{2,1,0:T(8,128)(2,1)S(1)} async-done(((bf16[16,32,128]{2,1,0:T(8,128)(2,1)}), bf16[16,32,128]{2,1,0:T(8,128)(2,1)S(1)}, u32[]{:S(2)}, u32[]{:S(2)}) %all-to-all-start.1) | async-done | bytes 131104 | tf_op jit(solution)/shard_map/all_to_all | solution.py:278
  74.9 0.0 copy-start.1
  74.9 0.7 copy-done.1
  75.5 13.1 %pairs.1 = f32[16,32,128]{2,1,0:T(8,128)} custom-call(s32[272]{0:T(512)} %get-tuple-element.16.list_ref, s32[1]{0:T(128)} %get-tuple-element.17.count_ref, bf16[16,32,128]{2,1,0:T(8,128)(2,1)} %copy-done, bf16[16,32,128]{2,1,0:T(8,128)(2,1)} %copy-done.1, bf16[16,32,128]{2,1,0:T(8,128)(2,1)} %all_to_all.20.tr_ref), custom_call_target="tpu_custom_call" | custom-call | tf_op jit(solution)/shard_map/pairs/pallas_call | solution.py:325
  88.7 17.0 %all_to_all.21.part_ref = f32[16,32,128]{2,1,0:T(8,128)} all-to-all(f32[16,32,128]{2,1,0:T(8,128)} %pairs.1), channel_id=1, replica_groups=mesh['x'=4,'zl'=2,'core'=2,'zh'=4,'y'=4] {'zl','core','zh'}, dimensions={0} | all-to-all | bytes 524288 | tf_op jit(solution)/shard_map/all_to_all | solution.py:340
  105.6 2.0 %finish.1 = (f32[32,2,8,128]{3,2,1,0:T(8,128)}, f32[32,128]{1,0:T(8,128)}) custom-call(f32[16,32,128]{2,1,0:T(8,128)} %all_to_all.21.part_ref, f32[32,2,8,128]{3,2,1,0:T(8,128)} %get-tuple-element.27.rel_ref, s32[1,128]{1,0:T(1,128)} %bitcast.5), custom_call_target="tpu_custom_call" | custom-call | tf_op jit(solution)/shard_map/finish/pallas_call | solution.py:341
Async XLA Ops:
  4.5 33.1 %all-to-all-start = ((bf16[16,32,128]{2,1,0:T(8,128)(2,1)}), bf16[16,32,128]{2,1,0:T(8,128)(2,1)S(1)}, u32[]{:S(2)}, u32[]{:S(2)}) async-start(bf16[16,32,128]{2,1,0:T(8,128)(2,1)} %broadcast_in_dim.10), calls=%async_computation | async-start | bytes 262144 | tf_op jit(solution)/shard_map/all_to_all | solution.py:278
  13.8 20.8 %collective-permute-start = (bf16[32,8,128]{2,1,0:T(8,128)(2,1)}, bf16[32,8,128]{2,1,0:T(8,128)(2,1)S(1)}, u32[]{:S(2)}, u32[]{:S(2)}) collective-permute-start(bf16[32,8,128]{2,1,0:T(8,128)(2,1)} %get-tuple-element.20), channel_id=1, source_target_pairs={{0,16},{16,32},{32,48},{48,64},{64,80},{80,96},{96,112},{112,128},... | collective-permute-start | bytes 196616 | tf_op jit(solution)/shard_map/ppermute | solution.py:274
  18.2 16.4 %collective-permute-start.1 = (bf16[32,8,128]{2,1,0:T(8,128)(2,1)}, bf16[32,8,128]{2,1,0:T(8,128)(2,1)S(1)}, u32[]{:S(2)}, u32[]{:S(2)}) collective-permute-start(bf16[32,8,128]{2,1,0:T(8,128)(2,1)} %get-tuple-element.21), channel_id=1, source_target_pairs={{16,0},{32,16},{48,32},{64,48},{80,64},{96,80},{112,96},{128,112},... | collective-permute-start | bytes 196616 | tf_op jit(solution)/shard_map/ppermute | solution.py:274
  20.1 9.8 %collective-permute-start.2 = (bf16[64,128]{1,0:T(8,128)(2,1)}, bf16[64,128]{1,0:T(8,128)(2,1)S(1)}, u32[]{:S(2)}, u32[]{:S(2)}) collective-permute-start(bf16[64,128]{1,0:T(8,128)(2,1)} %get-tuple-element.22), channel_id=1, source_target_pairs={{0,4},{4,8},{8,12},{1,5},{5,9},{9,13},{2,6},{6,10},{10,14},{3,7},{... | collective-permute-start | bytes 49160 | tf_op jit(solution)/shard_map/ppermute | solution.py:274
  25.0 6.5 %collective-permute-start.3 = (bf16[64,128]{1,0:T(8,128)(2,1)}, bf16[64,128]{1,0:T(8,128)(2,1)S(1)}, u32[]{:S(2)}, u32[]{:S(2)}) collective-permute-start(bf16[64,128]{1,0:T(8,128)(2,1)} %get-tuple-element.23), channel_id=1, source_target_pairs={{4,0},{8,4},{12,8},{5,1},{9,5},{13,9},{6,2},{10,6},{14,10},{7,3},{... | collective-permute-start | bytes 49160 | tf_op jit(solution)/shard_map/ppermute | solution.py:274
  26.3 5.3 %collective-permute-start.4 = (bf16[16,512]{1,0:T(8,128)(2,1)}, bf16[16,512]{1,0:T(8,128)(2,1)S(1)}, u32[]{:S(2)}, u32[]{:S(2)}) collective-permute-start(bf16[16,512]{1,0:T(8,128)(2,1)} %get-tuple-element.24), channel_id=1, source_target_pairs={{0,1},{1,2},{2,3},{4,5},{5,6},{6,7},{8,9},{9,10},{10,11},{12,13},{... | collective-permute-start | bytes 49160 | tf_op jit(solution)/shard_map/ppermute | solution.py:274
  29.9 4.7 %copy-start.4 = (bf16[64,128]{1,0:T(8,128)(2,1)}, bf16[64,128]{1,0:T(8,128)(2,1)S(1)}, u32[]{:S(2)}) copy-start(bf16[64,128]{1,0:T(8,128)(2,1)S(1)} %collective-permute-done.2.yl_ref) | copy-start | bytes 49156
  29.9 4.7 %collective-permute-start.5 = (bf16[16,512]{1,0:T(8,128)(2,1)}, bf16[16,512]{1,0:T(8,128)(2,1)S(1)}, u32[]{:S(2)}, u32[]{:S(2)}) collective-permute-start(bf16[16,512]{1,0:T(8,128)(2,1)} %get-tuple-element.25), channel_id=1, source_target_pairs={{1,0},{2,1},{3,2},{5,4},{6,5},{7,6},{9,8},{10,9},{11,10},{13,12},{... | collective-permute-start | bytes 49160 | tf_op jit(solution)/shard_map/ppermute | solution.py:274
  31.6 3.1 %copy-start.5 = (bf16[64,128]{1,0:T(8,128)(2,1)}, bf16[64,128]{1,0:T(8,128)(2,1)S(1)}, u32[]{:S(2)}) copy-start(bf16[64,128]{1,0:T(8,128)(2,1)S(1)} %collective-permute-done.3.yh_ref) | copy-start | bytes 49156
  31.6 3.1 %copy-start.6 = (bf16[16,512]{1,0:T(8,128)(2,1)}, bf16[16,512]{1,0:T(8,128)(2,1)S(1)}, u32[]{:S(2)}) copy-start(bf16[16,512]{1,0:T(8,128)(2,1)S(1)} %collective-permute-done.4.zl_ref) | copy-start | bytes 49156
  34.6 0.6 copy-start.7
  34.6 0.6 copy-start.2
  34.6 0.6 copy-start.3
  37.5 13.8 %copy-start = (bf16[16,32,128]{2,1,0:T(8,128)(2,1)}, bf16[16,32,128]{2,1,0:T(8,128)(2,1)S(1)}, u32[]{:S(2)}) copy-start(bf16[16,32,128]{2,1,0:T(8,128)(2,1)S(1)} %all-to-all-done.src_ref) | copy-start | bytes 393220
  38.3 13.1 %copy-start.8 = (bf16[32,128]{1,0:T(8,128)(2,1)S(1)}, bf16[32,128]{1,0:T(8,128)(2,1)}, u32[]{:S(2)}) copy-start(bf16[32,128]{1,0:T(8,128)(2,1)} %get-tuple-element.19) | copy-start | bytes 24580
  52.0 22.9 %all-to-all-start.1 = ((bf16[16,32,128]{2,1,0:T(8,128)(2,1)}), bf16[16,32,128]{2,1,0:T(8,128)(2,1)S(1)}, u32[]{:S(2)}, u32[]{:S(2)}) async-start(bf16[16,32,128]{2,1,0:T(8,128)(2,1)} %broadcast_in_dim.11), calls=%async_computation.1 | async-start | bytes 262144 | tf_op jit(solution)/shard_map/all_to_all | solution.py:278
  74.9 0.7 copy-start.1
